TPU v7x, 256 devices: a whole 4x4x8 slice. The times are simulated.
256 devices in a mesh: chan: 8 (over x, core), filt: 32 (over y, z).
Axes of the slice: x: 4, y: 4, z: 8, core: 2. Of those that a mesh axis runs over, the one named last changes fastest.
Arguments:
- inputs: bfloat16 [1, 64, 128, 1024], P(None, 'filt', None, 'chan'), may hold values from -6 to 6
- weights: bfloat16 [3, 3, 1024, 1024], P(None, None, 'filt', 'chan'), may hold values from -0.0625 to 0.0625
- cotangent: bfloat16 [1, 64, 1024, 128], P(None, 'chan', 'filt'), may hold values from -6 to 6
Outputs:
- outputs: bfloat16 [1, 64, 1024, 128], P(None, 'chan', 'filt')
- input_grad: bfloat16 [1, 64, 128, 1024], P(None, 'filt', None, 'chan')
- weight_grad: float32 [3, 3, 1024, 1024], P(None, None, 'filt', 'chan')
All inputs are finite; a program needn't handle non-finite values.
Results may differ from a plain program's by a relative error of at most 0.001.
Values may be sent and summed in bfloat16 or wider, within the bound.
A program may use at most 128 MiB of HBM per device.

v0:
```python
import math
import jax
import jax.numpy as jnp
from jax import lax
from jax.sharding import PartitionSpec as P


def backward_taps(padded, kernel, row_count, col_count):
    summed = None
    for tap_row in range(3):
        for tap_col in range(3):
            source = padded[
                :, 2 - tap_row : 2 - tap_row + row_count, :, 2 - tap_col : 2 - tap_col + col_count
            ]
            product = jnp.einsum(
                "bhfw,fc->bhwc",
                source,
                kernel[tap_row, tap_col],
                preferred_element_type=jnp.float32,
            )
            summed = product if summed is None else summed + product
    return summed


def body(inputs, weights, cotangent):
    gathered = lax.all_gather(inputs, "filt", axis=1, tiled=True)
    cot_all = lax.all_gather(cotangent, "chan", axis=1, tiled=True)
    row_count = gathered.shape[1]
    col_count = gathered.shape[2]
    padded_in = jnp.pad(gathered, ((0, 0), (1, 1), (1, 1), (0, 0)))
    norm_factor = 1.0 / math.sqrt(gathered.shape[0] * row_count * col_count)
    summed_out = None
    grad_taps = []
    for tap_row in range(3):
        for tap_col in range(3):
            source = padded_in[:, tap_row : tap_row + row_count, tap_col : tap_col + col_count, :]
            product = jnp.einsum(
                "bhwc,fc->bhwf",
                source,
                weights[tap_row, tap_col],
                preferred_element_type=jnp.float32,
            )
            summed_out = product if summed_out is None else summed_out + product
            grad_taps.append(
                jnp.einsum("bhwc,bhfw->fc", source, cot_all, preferred_element_type=jnp.float32)
                * norm_factor
            )
    partial_out = jnp.transpose(summed_out, (0, 1, 3, 2))
    outputs = lax.psum_scatter(partial_out, "chan", scatter_dimension=1, tiled=True).astype(
        jnp.bfloat16
    )
    weight_grad = jnp.stack(grad_taps).reshape(3, 3, weights.shape[2], weights.shape[3])
    padded_cot = jnp.pad(cot_all, ((0, 0), (1, 1), (0, 0), (1, 1)))
    partial_grad = backward_taps(padded_cot, weights, row_count, col_count)
    input_grad = lax.psum_scatter(partial_grad, "filt", scatter_dimension=1, tiled=True).astype(
        jnp.bfloat16
    )
    return (outputs, input_grad, weight_grad)


def solution(mesh):
    return jax.shard_map(
        body,
        mesh=mesh,
        in_specs=(
            P(None, "filt", None, "chan"),
            P(None, None, "filt", "chan"),
            P(None, "chan", "filt", None),
        ),
        out_specs=(
            P(None, "chan", "filt", None),
            P(None, "filt", None, "chan"),
            P(None, None, "filt", "chan"),
        ),
        check_vma=False,
    )
```

profile of v0, /device:TPU:2, one launch (start us, length us, event | category | flops | bytes accessed | tf_op | source)
XLA Modules:
  0.0 368.4 jit_solution(7794976326158176993)
XLA Ops:
  7.2 0.0 all-gather.2.cloned.1.call-start
  7.2 0.7 all-gather.2.cloned.1.call-update
  7.9 0.0 reduce-scatter.3.cloned.1.call-start
  7.9 13.4 %all_gather.7 = bf16[1,64,32,128]{3,2,0,1:T(8,128)(2,1)S(1)} all-gather(bf16[1,8,32,128]{3,2,0,1:T(8,128)(2,1)} %bitcast.402), channel_id=1, replica_groups=mesh['chan'=8,'filt'=32] {'chan'}, dimensions={1}, use_global_device_ids=true | all-gather | bytes 589824 | tf_op jit(solution)/shard_map/all_gather | solution.py:27
  21.3 0.0 copy-start.4
  21.3 3.8 %fusion.188 = f32[64,128,128]{2,1,0:T(8,128)} fusion(bf16[1,64,32,128]{3,2,1,0:T(8,128)(2,1)S(1)} %bitcast.394, bf16[3,3,32,128]{3,2,1,0:T(8,128)(2,1)} %param.4), kind=kOutput, calls=%fused_computation.107 | convolution fusion | flops 67108864 | bytes 4726784 | tf_op jit(solution)/shard_map/bhfw,fc->bhwc/dot_general | solution.py:15
  25.1 0.0 copy-done.4
  25.1 2.7 fusion.191
  27.8 3.0 fusion.194
  30.8 3.0 fusion.197
  33.9 3.0 fusion.200
  36.9 54.9 %all-gather.2.cloned.1.call-done = bf16[1,64,128,128]{3,2,0,1:T(8,128)(2,1)} async-done(((bf16[1,2,128,128]{3,2,0,1:T(8,128)(2,1)}), bf16[1,64,128,128]{3,2,0,1:T(8,128)(2,1)}) %all-gather.2.cloned.1.call-update) | async-done | bytes 2097168 | tf_op jit(solution)/shard_map/all_gather | solution.py:26
  91.8 0.0 copy-start
  91.8 2.5 fusion.26
  94.3 0.0 copy-done
  94.3 0.8 fusion.30
  95.1 0.8 fusion.10
  96.0 0.8 fusion.2
  96.8 0.8 fusion.55
  97.6 0.8 fusion.18
  98.4 0.8 fusion.61
  99.3 0.8 fusion.67
  100.1 1.8 fusion.76
  102.0 0.0 reduce-scatter.3.cloned.1.call-update
  102.0 0.2 reduce-scatter.5.cloned.1.call-start
  102.2 0.0 copy-start.3
  102.2 3.0 fusion.203
  105.2 0.0 copy-start.2
  105.2 2.7 fusion.206
  108.0 0.0 copy-start.1
  108.0 2.7 fusion.219
  110.7 0.0 copy-done.3
  110.7 0.0 copy-done.2
  110.7 0.7 copy-done.1
  111.4 10.6 %add_bitcast_fusion = f32[1,64,128,128]{3,2,1,0:T(8,128)} fusion(f32[64,128,128]{2,1,0:T(8,128)} %fusion.206, f32[64,128,128]{2,1,0:T(8,128)} %fusion.203, f32[64,128,128]{2,1,0:T(8,128)} %fusion.200, f32[64,128,128]{2,1,0:T(8,128)} %fusion.219, f32[64,128,128]{2,1,0:T(8,128)} %fusion.197, f32[64,128,128]{2,1,0:T(8,128)S(1)} %copy-done.3, ...), kind=kOutput, calls=%fused_computation | convolution fusion | flops 75497472 | bytes 38281216 | tf_op jit(solution)/shard_map/bhfw,fc->bhwc/dot_general | solution.py:15
  122.0 0.0 reduce-scatter.5.cloned.1.call-update
  122.0 0.7 fusion.175
  122.7 0.5 fusion.166
  123.2 0.8 fusion.157
  124.0 0.8 fusion.148
  124.8 0.5 fusion.184
  125.2 0.8 fusion.139
  126.0 0.8 fusion.130
  126.8 0.5 fusion.121
  127.3 0.8 fusion.112
  128.0 0.0 copy-start.5
  128.0 2.8 reduce-scatter.3.cloned.1.call-done
  130.9 1.5 convert_element_type.10
  132.4 227.9 %reduce-scatter.5.cloned.1.call-done = f32[1,2,128,128]{3,2,1,0:T(8,128)} async-done(((f32[1,64,128,128]{3,2,1,0:T(8,128)}), f32[1,2,128,128]{3,2,1,0:T(8,128)}) %reduce-scatter.5.cloned.1.call-update) | async-done | bytes 131088 | tf_op jit(solution)/shard_map/reduce_scatter | solution.py:55
  360.3 1.5 convert_element_type.11
  361.9 0.0 copy-done.5
Async XLA Ops:
  7.2 84.6 %all-gather.2.cloned.1.call-start = ((), (), s32[]{:S(2)}) async-start(), calls=%async_computation.2 | async-start | bytes 2162688 | tf_op jit(solution)/shard_map/all_gather | solution.py:26
  7.9 123.0 %reduce-scatter.3.cloned.1.call-start = ((), (), s32[]{:S(2)}) async-start(), calls=%async_computation.3 | async-start | bytes 1179648 | tf_op jit(solution)/shard_map/reduce_scatter | solution.py:49
  21.3 3.8 %copy-start.4 = (bf16[3,3,32,128]{3,2,1,0:T(8,128)(2,1)S(1)}, bf16[3,3,32,128]{3,2,1,0:T(8,128)(2,1)}, u32[]{:S(2)}) copy-start(bf16[3,3,32,128]{3,2,1,0:T(8,128)(2,1)} %param.4) | copy-start | bytes 221188
  91.8 2.6 copy-start
  102.0 258.3 %reduce-scatter.5.cloned.1.call-start = ((), (), s32[]{:S(2)}) async-start(), calls=%async_computation.4 | async-start | bytes 4325376 | tf_op jit(solution)/shard_map/reduce_scatter | solution.py:55
  102.2 8.5 %copy-start.3 = (f32[64,128,128]{2,1,0:T(8,128)S(1)}, f32[64,128,128]{2,1,0:T(8,128)}, u32[]{:S(2)}) copy-start(f32[64,128,128]{2,1,0:T(8,128)} %fusion.194) | copy-start | bytes 12582916
  105.2 5.5 %copy-start.2 = (f32[64,128,128]{2,1,0:T(8,128)S(1)}, f32[64,128,128]{2,1,0:T(8,128)}, u32[]{:S(2)}) copy-start(f32[64,128,128]{2,1,0:T(8,128)} %fusion.191) | copy-start | bytes 12582916
  108.0 3.4 copy-start.1
  128.0 233.9 %copy-start.5 = (f32[9,32,128]{2,1,0:T(8,128)}, f32[9,32,128]{2,1,0:T(8,128)S(1)}, u32[]{:S(2)}) copy-start(f32[9,32,128]{2,1,0:T(8,128)S(1)} %fusion.112) | copy-start | bytes 442372
Sparse Core Ops, SparseCore 0:
  10.6 81.1 all-gather.1
  102.1 28.7 reduce-scatter.2
  134.8 225.5 reduce-scatter.4
where the time goes:
time: 369 us; the launch traced here: 368 us
  waiting for transfers between devices  286 us (78%)
  matrix products  50.8 us (14%)
  between operations  13.8 us (4%)
  blocking collectives  13.4 us (4%)
    reduce_scatter x1, waiting for transfers between devices, body(): lax.psum_scatter(partial_grad, 'filt', scatter_dimension=1, tiled=True)  228 us
    all_gather x1, waiting for transfers between devices, body(): gathered = lax.all_gather(inputs, 'filt', axis=1, tiled=True)  54.9 us
    dot_general x9, matrix products, backward_taps(): jnp.einsum('bhfw,fc->bhwc', source, kernel[tap_row, tap_col], preferred_e...  34.6 us
    all_gather x1, blocking collectives, body(): cot_all = lax.all_gather(cotangent, 'chan', axis=1, tiled=True)  13.4 us
    dot_general x9, matrix products, body(): jnp.einsum('bhwc,fc->bhwf', source, weights[tap_row, tap_col], preferred_...  10.2 us
  transfers between devices with their start and end apart: 3, of which 3 were waited for; matrix products, arithmetic and copies ran while one was open for 11% of the time, Pallas kernels for 0%

commit v1 on v0

--- a/solution.py
+++ b/solution.py
@@ -23,7 +23,9 @@
 
 
 def body(inputs, weights, cotangent):
-    gathered = lax.all_gather(inputs, "filt", axis=1, tiled=True)
+    gathered = jnp.concatenate(
+        lax.all_to_all(jnp.stack([inputs] * lax.axis_size("filt")), "filt", 0, 0), axis=1
+    )
     cot_all = lax.all_gather(cotangent, "chan", axis=1, tiled=True)
     row_count = gathered.shape[1]
     col_count = gathered.shape[2]

time: 369 us -> 348 us (0.943)
  waiting for transfers between devices: 286 us -> 254 us
  starting transfers between devices: 0.3 us -> 11.9 us
    all_gather x1 -> x0, waiting for transfers between devices: 54.9 us -> none  [body(): gathered = lax.all_gather(inputs, 'filt', axis=1, tiled=True)]
    all_to_all x0 -> x1, waiting for transfers between devices: none -> 22.1 us  [body(): lax.all_to_all(jnp.stack([inputs] * lax.axis_size('filt')), 'filt', 0, 0)]
    all_to_all x0 -> x1, starting transfers between devices: none -> 11.6 us  [body(): lax.all_to_all(jnp.stack([inputs] * lax.axis_size('filt')), 'filt', 0, 0)]
  transfers between devices with their start and end apart: 3 -> 3, of which waited for: 3 -> 3; matrix products, arithmetic and copies ran while one was open for 11% -> 12% of each run, Pallas kernels for 0% -> 0%
where the time goes in v1:
time: 348 us; the launch traced here: 347 us
  waiting for transfers between devices  254 us (73%)
  matrix products  48.3 us (14%)
  between operations  14.1 us (4%)
  blocking collectives  13.2 us (4%)
  starting transfers between devices  11.9 us (3%)
    reduce_scatter x1, waiting for transfers between devices, body(): lax.psum_scatter(partial_grad, 'filt', scatter_dimension=1, tiled=True)  228 us
    dot_general x9, matrix products, backward_taps(): jnp.einsum('bhfw,fc->bhwc', source, kernel[tap_row, tap_col], preferred_e...  33.9 us
    all_to_all x1, waiting for transfers between devices, body(): lax.all_to_all(jnp.stack([inputs] * lax.axis_size('filt')), 'filt', 0, 0)  22.1 us
    all_gather x1, blocking collectives, body(): cot_all = lax.all_gather(cotangent, 'chan', axis=1, tiled=True)  13.2 us
    all_to_all x1, starting transfers between devices, body(): lax.all_to_all(jnp.stack([inputs] * lax.axis_size('filt')), 'filt', 0, 0)  11.6 us
    dot_general x9, matrix products, body(): jnp.einsum('bhwc,fc->bhwf', source, weights[tap_row, tap_col], preferred_...  8.45 us
  transfers between devices with their start and end apart: 3, of which 3 were waited for; matrix products, arithmetic and copies ran while one was open for 12% of the time, Pallas kernels for 0%

profile of v1, /device:TPU:2, one launch (start us, length us, event | category | flops | bytes accessed | tf_op | source)
XLA Modules:
  0.0 347.5 jit_solution(17322843580735847765)
XLA Ops:
  7.2 2.7 stack.22
  9.9 0.0 copy-start.4
  9.9 0.0 copy-start.3
  9.9 11.6 %all-to-all-start = ((bf16[32,1,2,128,128]{4,3,2,1,0:T(8,128)(2,1)}), bf16[32,1,2,128,128]{4,3,2,1,0:T(8,128)(2,1)S(1)}, u32[]{:S(2)}, u32[]{:S(2)}) async-start(bf16[32,1,2,128,128]{4,3,2,1,0:T(8,128)(2,1)} %stack.22), calls=%async_computation | async-start | bytes 4194304 | tf_op jit(solution)/shard_map/all_to_all | solution.py:27
  21.5 0.0 reduce-scatter.3.cloned.1.call-start
  21.5 0.0 copy-done.4
  21.5 13.2 %all_gather.3 = bf16[1,64,32,128]{3,2,0,1:T(8,128)(2,1)S(1)} all-gather(bf16[1,8,32,128]{3,2,0,1:T(8,128)(2,1)S(1)} %bitcast.395), channel_id=1, replica_groups=mesh['chan'=8,'filt'=32] {'chan'}, dimensions={1}, use_global_device_ids=true | all-gather | bytes 589824 | tf_op jit(solution)/shard_map/all_gather | solution.py:29
  34.7 0.0 copy-done.3
  34.7 3.0 fusion.175
  37.7 2.7 fusion.178
  40.4 3.0 fusion.181
  43.4 3.0 fusion.184
  46.5 3.0 fusion.187
  49.5 22.1 %all-to-all-done = bf16[32,1,2,128,128]{4,3,2,1,0:T(8,128)(2,1)S(1)} async-done(((bf16[32,1,2,128,128]{4,3,2,1,0:T(8,128)(2,1)}), bf16[32,1,2,128,128]{4,3,2,1,0:T(8,128)(2,1)S(1)}, u32[]{:S(2)}, u32[]{:S(2)}) %all-to-all-start) | async-done | bytes 2097184 | tf_op jit(solution)/shard_map/all_to_all | solution.py:27
  71.5 0.8 fusion.22
  72.3 0.8 fusion.26
  73.2 0.8 fusion.10
  74.0 0.8 fusion.2
  74.8 0.8 fusion.217
  75.6 0.8 fusion.51
  76.5 0.8 fusion.57
  77.3 0.8 fusion.63
  78.2 1.8 fusion.72
  80.0 0.0 reduce-scatter.3.cloned.1.call-update
  80.0 0.2 reduce-scatter.5.cloned.1.call-start
  80.2 0.0 copy-start.2
  80.3 3.0 fusion.190
  83.2 0.0 copy-start.1
  83.2 2.7 fusion.193
  86.0 0.0 copy-start
  86.0 2.7 fusion.206
  88.7 0.0 copy-done.2
  88.7 0.0 copy-done.1
  88.7 0.6 copy-done
  89.4 10.6 %add_bitcast_fusion = f32[1,64,128,128]{3,2,1,0:T(8,128)} fusion(f32[64,128,128]{2,1,0:T(8,128)} %fusion.193, f32[64,128,128]{2,1,0:T(8,128)} %fusion.190, f32[64,128,128]{2,1,0:T(8,128)} %fusion.187, f32[64,128,128]{2,1,0:T(8,128)} %fusion.206, f32[64,128,128]{2,1,0:T(8,128)} %fusion.184, f32[64,128,128]{2,1,0:T(8,128)S(1)} %copy-done.2, ...), kind=kOutput, calls=%fused_computation | convolution fusion | flops 75497472 | bytes 38281216 | tf_op jit(solution)/shard_map/bhfw,fc->bhwc/dot_general | solution.py:15
  100.0 0.0 reduce-scatter.5.cloned.1.call-update
  100.0 0.7 fusion.171
  100.7 0.5 fusion.162
  101.2 0.8 fusion.153
  102.0 0.8 fusion.144
  102.8 0.5 fusion.101
  103.2 0.8 fusion.135
  104.0 0.8 fusion.126
  104.8 0.5 fusion.117
  105.3 0.8 fusion.108
  106.0 0.0 copy-start.5
  106.0 3.4 reduce-scatter.3.cloned.1.call-done
  109.5 1.5 convert_element_type.10
  111.0 228.1 %reduce-scatter.5.cloned.1.call-done = f32[1,2,128,128]{3,2,1,0:T(8,128)} async-done(((f32[1,64,128,128]{3,2,1,0:T(8,128)}), f32[1,2,128,128]{3,2,1,0:T(8,128)}) %reduce-scatter.5.cloned.1.call-update) | async-done | bytes 131088 | tf_op jit(solution)/shard_map/reduce_scatter | solution.py:57
  339.1 1.5 convert_element_type.11
  340.6 0.0 copy-done.5
Async XLA Ops:
  9.9 11.7 %copy-start.4 = (bf16[1,8,32,128]{3,2,1,0:T(8,128)(2,1)S(1)}, bf16[1,8,32,128]{3,2,1,0:T(8,128)(2,1)}, u32[]{:S(2)}) copy-start(bf16[1,8,32,128]{3,2,1,0:T(8,128)(2,1)} %param.5) | copy-start | bytes 196612
  9.9 24.9 %copy-start.3 = (bf16[3,3,32,128]{3,2,1,0:T(8,128)(2,1)S(1)}, bf16[3,3,32,128]{3,2,1,0:T(8,128)(2,1)}, u32[]{:S(2)}) copy-start(bf16[3,3,32,128]{3,2,1,0:T(8,128)(2,1)} %param.4) | copy-start | bytes 221188
  9.9 61.7 %all-to-all-start = ((bf16[32,1,2,128,128]{4,3,2,1,0:T(8,128)(2,1)}), bf16[32,1,2,128,128]{4,3,2,1,0:T(8,128)(2,1)S(1)}, u32[]{:S(2)}, u32[]{:S(2)}) async-start(bf16[32,1,2,128,128]{4,3,2,1,0:T(8,128)(2,1)} %stack.22), calls=%async_computation | async-start | bytes 4194304 | tf_op jit(solution)/shard_map/all_to_all | solution.py:27
  21.5 88.0 %reduce-scatter.3.cloned.1.call-start = ((), (), s32[]{:S(2)}) async-start(), calls=%async_computation.3 | async-start | bytes 1179648 | tf_op jit(solution)/shard_map/reduce_scatter | solution.py:51
  80.0 259.1 %reduce-scatter.5.cloned.1.call-start = ((), (), s32[]{:S(2)}) async-start(), calls=%async_computation.4 | async-start | bytes 4325376 | tf_op jit(solution)/shard_map/reduce_scatter | solution.py:57
  80.2 8.5 %copy-start.2 = (f32[64,128,128]{2,1,0:T(8,128)S(1)}, f32[64,128,128]{2,1,0:T(8,128)}, u32[]{:S(2)}) copy-start(f32[64,128,128]{2,1,0:T(8,128)} %fusion.181) | copy-start | bytes 12582916
  83.2 5.5 %copy-start.1 = (f32[64,128,128]{2,1,0:T(8,128)S(1)}, f32[64,128,128]{2,1,0:T(8,128)}, u32[]{:S(2)}) copy-start(f32[64,128,128]{2,1,0:T(8,128)} %fusion.178) | copy-start | bytes 12582916
  86.0 3.4 copy-start
  106.0 234.6 %copy-start.5 = (f32[9,32,128]{2,1,0:T(8,128)}, f32[9,32,128]{2,1,0:T(8,128)S(1)}, u32[]{:S(2)}) copy-start(f32[9,32,128]{2,1,0:T(8,128)S(1)} %fusion.108) | copy-start | bytes 442372
Sparse Core Ops, SparseCore 0:
  80.1 29.2 reduce-scatter.2
  113.4 225.6 reduce-scatter.4
